TPU v7x, 256 devices: a whole 4x4x8 slice. The times are simulated.
256 devices in a mesh: bubble: 16 (over y_hi, z), panel: 16 (over y_lo, x, core).
Axes of the slice: x: 4, y: 4 (y_hi: 2, y_lo: 2; y = y_hi * 2 + y_lo), z: 8, core: 2. Of those that a mesh axis runs over, the one named last changes fastest.
Arguments:
- density: float32 [128, 12288], P('bubble', 'panel'), may hold values from -6 to 6
- right_side: float32 [128, 12288], P('bubble', 'panel'), may hold values from -6 to 6
- inv_diag: bfloat16 [128, 96, 128, 128], P('bubble', 'panel')
- near_vals: bfloat16 [128, 96, 4, 128, 128], P('bubble', 'panel'), may hold values from -0.25 to 0.25
- near_bubble: int32 [128, 96, 4], P('bubble', 'panel'), may hold values from 0 to 127, as said below
- near_block: int32 [128, 96, 4], P('bubble', 'panel'), may hold values from 0 to 95
- near_count: int32 [128, 96], P('bubble', 'panel'), may hold values from 1 to 4, as said below
- colour: int32 [128], P('bubble'), may hold values from 0 to 1
- moment_map: bfloat16 [128, 16, 12288], P('bubble', None, 'panel'), may hold values from -0.0546875 to 0.0546875
- spread_map: bfloat16 [128, 16, 12288], P('bubble', None, 'panel'), may hold values from -0.125 to 0.125
- centres: float32 [3, 128], replicated, may hold values from 0.2 to 6
Outputs:
- relaxed: float32 [128, 12288], P('bubble', 'panel')
Inputs may be any that keep to these rules, and one draw needn't show every extreme that they name: `near_bubble`: every slot of bubble b names a bubble within 8 of b. `near_count`: the first row block of every bubble uses all 4 slots.
All inputs are finite; a program needn't handle non-finite values.
Results may differ from a plain program's by a relative error of at most 0.0041.
Values may be sent and summed in bfloat16 or wider, within the bound.
No kernel may reach another device: no remote copies, remote signals or barrier semaphores. Data moves between devices by JAX's collectives and lax.ppermute only.
A program may use at most 64 MiB of HBM per device.

v0:
```python
import jax
import jax.numpy as jnp
from jax import lax
from jax.sharding import PartitionSpec as P


def with_halo(shard, sides, width):
    for axis, dim in sides:
        peers, length = (lax.axis_size(axis), shard.shape[dim])
        up = [(i, (i + 1) % peers) for i in range(peers - 1)]
        down = [(j, i) for i, j in up]
        last = lax.slice_in_dim(shard, length - width, length, axis=dim)
        first = lax.slice_in_dim(shard, 0, width, axis=dim)
        before = lax.ppermute(last, axis, up)
        after = lax.ppermute(first, axis, down)
        shard = jnp.concatenate([before, shard, after], axis=dim)
    return shard


def near_field(
    neighbourhood, near_vals, near_bubble, near_block, near_count, first_bubble, block_size
):
    rim_count = neighbourhood.shape[0]
    blocks = neighbourhood.reshape(rim_count, neighbourhood.shape[1] // block_size, block_size)
    local_bubble = near_bubble - first_bubble
    sources = blocks[local_bubble, near_block]
    live_slot = jnp.arange(near_vals.shape[2])[None, None, :] < near_count[:, :, None]
    sources = jnp.where(live_slot[:, :, :, None], sources, jnp.zeros_like(sources))
    return jnp.einsum("brsij,brsj->bri", near_vals, sources, preferred_element_type=jnp.float32)


def far_kernel(centres, my_bubbles, reach):
    centre_mine = centres[:, my_bubbles]
    diff = centre_mine[:, :, None] - centres[:, None, :]
    direct_sq = jnp.sum(diff * diff, axis=0)
    mirrored = centre_mine[2][:, None] + centres[2][None, :]
    image_sq = diff[0] * diff[0] + diff[1] * diff[1] + mirrored * mirrored
    kernel = 1.0 / jnp.sqrt(direct_sq + 1.0) + 1.0 / jnp.sqrt(image_sq + 1.0)
    gap = jnp.abs(my_bubbles[:, None] - jnp.arange(centres.shape[1])[None, :])
    return jnp.where(gap > reach, kernel, jnp.zeros_like(kernel))


def per_device(
    density,
    right_side,
    inv_diag,
    near_vals,
    near_bubble,
    near_block,
    near_count,
    colour,
    moment_map,
    spread_map,
    centres,
):
    bub_dev = density.shape[0]
    panels_dev = density.shape[1]
    block_size = inv_diag.shape[2]
    my_index = lax.axis_index("bubble")
    my_bubbles = my_index * bub_dev + jnp.arange(bub_dev, dtype=jnp.int32)
    first_bubble = my_index * bub_dev - bub_dev
    kernel = far_kernel(centres, my_bubbles, bub_dev)
    relaxed = density
    for colour_now in range(2):
        dens_bf = relaxed.astype(jnp.bfloat16)
        panel_full = lax.all_gather(dens_bf, "panel", axis=1, tiled=True)
        neighbourhood = with_halo(panel_full, (("bubble", 0),), bub_dev)
        near = near_field(
            neighbourhood, near_vals, near_bubble, near_block, near_count, first_bubble, block_size
        )
        partial_value = jnp.einsum(
            "bki,bi->bk", moment_map, dens_bf, preferred_element_type=jnp.float32
        )
        own_moments = lax.psum(partial_value, "panel")
        all_moments = lax.all_gather(own_moments, "bubble", axis=0, tiled=True)
        far_coeff = jnp.dot(kernel, all_moments, precision=lax.Precision.HIGHEST).astype(
            jnp.bfloat16
        )
        far = jnp.einsum("bki,bk->bi", spread_map, far_coeff, preferred_element_type=jnp.float32)
        remainder = (right_side - near.reshape(bub_dev, panels_dev) - far).astype(jnp.bfloat16)
        remainder = remainder.reshape(bub_dev, panels_dev // block_size, block_size)
        updated = jnp.einsum(
            "brij,brj->bri", inv_diag, remainder, preferred_element_type=jnp.float32
        )
        relaxed = jnp.where(
            (colour == colour_now)[:, None], updated.reshape(bub_dev, panels_dev), relaxed
        )
    return relaxed


def solution(mesh):
    in_specs = (
        P("bubble", "panel"),
        P("bubble", "panel"),
        P("bubble", "panel", None, None),
        P("bubble", "panel", None, None, None),
        P("bubble", "panel", None),
        P("bubble", "panel", None),
        P("bubble", "panel"),
        P("bubble"),
        P("bubble", None, "panel"),
        P("bubble", None, "panel"),
        P(),
    )
    out_specs = P("bubble", "panel")
    return jax.shard_map(
        per_device, mesh=mesh, in_specs=in_specs, out_specs=out_specs, check_vma=False
    )
```

profile of v0, /device:TPU:24, one launch (start us, length us, event | category | flops | bytes accessed | tf_op | source)
XLA Modules:
  0.0 213.0 jit_solution(4248419762880765899)
XLA Ops:
  0.0 0.9 convert_element_type.18
  0.9 19.4 %all_gather.12 = bf16[8,12288]{1,0:T(8,128)(2,1)S(1)} all-gather(bf16[8,768]{1,0:T(8,128)(2,1)S(1)} %convert_element_type.18), channel_id=1, replica_groups=mesh['bubble'=16,'panel'=16] {'panel'}, dimensions={1}, use_global_device_ids=true | all-gather | bytes 208896 | tf_op jit(solution)/shard_map/all_gather | solution.py:66
  20.2 3.8 %collective-permute-start = (bf16[8,12288]{1,0:T(8,128)(2,1)S(1)}, bf16[8,12288]{1,0:T(8,128)(2,1)S(1)}, u32[]{:S(2)}, u32[]{:S(2)}) collective-permute-start(bf16[8,12288]{1,0:T(8,128)(2,1)S(1)} %all_gather.12), channel_id=1, source_target_pairs={{0,16},{16,32},{32,48},{48,64},{64,80},{80,96},{96,112},{112,128},... | collective-permute-start | bytes 589832 | tf_op jit(solution)/shard_map/ppermute | solution.py:14
  24.0 6.2 %collective-permute-start.1 = (bf16[8,12288]{1,0:T(8,128)(2,1)S(1)}, bf16[8,12288]{1,0:T(8,128)(2,1)S(1)}, u32[]{:S(2)}, u32[]{:S(2)}) collective-permute-start(bf16[8,12288]{1,0:T(8,128)(2,1)S(1)} %all_gather.12), channel_id=1, source_target_pairs={{16,0},{32,16},{48,32},{64,48},{80,64},{96,80},{112,96},{128,112},... | collective-permute-start | bytes 589832 | tf_op jit(solution)/shard_map/ppermute | solution.py:15
  30.3 0.8 copy.18
  31.1 0.6 gather_fusion.1
  31.7 0.1 copy.19
  31.8 0.2 slice_reduce_fusion
  31.9 0.7 slice_bitcast_fusion
  32.6 0.7 convert_bitcast_fusion
  33.4 0.8 multiply_reduce_fusion
  34.1 1.1 fusion.16
  35.2 27.2 %psum.14 = f32[8,16]{1,0:T(8,128)S(1)} all-reduce(f32[8,16]{1,0:T(8,128)S(1)} %bitcast.107), channel_id=1, replica_groups=mesh['bubble'=16,'panel'=16] {'panel'}, use_global_device_ids=true, to_apply=%region_1.2 | all-reduce | flops 128 | bytes 1024 | tf_op jit(solution)/shard_map/psum | solution.py:74
  62.4 37.8 %all_gather.13 = f32[128,16]{1,0:T(8,128)S(1)} all-gather(f32[8,16]{1,0:T(8,128)S(1)} %psum.14), channel_id=1, replica_groups=mesh['bubble'=16,'panel'=16] {'bubble'}, dimensions={0}, use_global_device_ids=true | all-gather | bytes 8704 | tf_op jit(solution)/shard_map/all_gather | solution.py:75
  100.2 0.7 fusion.22
  101.0 0.1 copy.17
  101.1 0.1 reshape.62
  101.2 0.8 iota_compare_fusion
  101.9 0.1 fusion.31
  102.0 0.2 fusion
  102.2 1.1 fusion.34
  103.3 0.7 broadcast_compare_fusion.1
  103.9 0.0 collective-permute-done
  103.9 0.0 collective-permute-done.1
  104.0 0.1 copy.36
  104.1 2.5 %gather_fusion = bf16[192,128]{1,0:T(8,128)(2,1)S(1)} fusion(bf16[24,96,128]{2,1,0:T(8,128)(2,1)S(1)} %bitcast.101, s32[192]{0:T(256)S(1)} %reshape.62), kind=kCustom, calls=%fused_computation | custom fusion | bytes 99840 | tf_op jit(solution)/shard_map/gather | solution.py:26
  106.6 0.1 select_bitcast_fusion.1
  106.7 0.0 copy-start.3
  106.8 4.5 %fusion.4 = f32[8,6,1,128,1]{3,2,4,1,0:T(1,128)S(1)} fusion(bf16[8,6,4,128,128]{4,3,2,1,0:T(8,128)(2,1)} %param.14, bf16[8,6,4,128,1]{3,2,1,0,4:T(4,128)(2,1)S(1)} %select_bitcast_fusion.1), kind=kOutput, calls=%fused_computation.11 | convolution fusion | flops 6291456 | bytes 6365184 | tf_op jit(solution)/shard_map/brsij,brsj->bri/dot_general | solution.py:29
  111.3 0.0 copy-start.1
  111.3 0.9 fusion.14
  112.2 0.1 fusion.36
  112.3 16.5 %all_gather.14 = bf16[8,12288]{1,0:T(8,128)(2,1)S(1)} all-gather(bf16[8,768]{1,0:T(8,128)(2,1)S(1)} %fusion.36), channel_id=1, replica_groups=mesh['bubble'=16,'panel'=16] {'panel'}, dimensions={1}, use_global_device_ids=true | all-gather | bytes 208896 | tf_op jit(solution)/shard_map/all_gather | solution.py:66
  128.8 2.0 collective-permute-start.2
  130.8 7.5 %collective-permute-start.3 = (bf16[8,12288]{1,0:T(8,128)(2,1)S(1)}, bf16[8,12288]{1,0:T(8,128)(2,1)S(1)}, u32[]{:S(2)}, u32[]{:S(2)}) collective-permute-start(bf16[8,12288]{1,0:T(8,128)(2,1)S(1)} %all_gather.14), channel_id=1, source_target_pairs={{16,0},{32,16},{48,32},{64,48},{80,64},{96,80},{112,96},{128,112},... | collective-permute-start | bytes 589832 | tf_op jit(solution)/shard_map/ppermute | solution.py:15
  138.3 0.2 fusion.12
  138.4 28.5 %psum.15 = f32[8,16]{1,0:T(8,128)S(1)} all-reduce(f32[8,16]{1,0:T(8,128)S(1)} %bitcast.108), channel_id=1, replica_groups=mesh['bubble'=16,'panel'=16] {'panel'}, use_global_device_ids=true, to_apply=%region_2.3 | all-reduce | flops 128 | bytes 1024 | tf_op jit(solution)/shard_map/psum | solution.py:74
  166.9 36.7 %all_gather.15 = f32[128,16]{1,0:T(8,128)S(1)} all-gather(f32[8,16]{1,0:T(8,128)S(1)} %psum.15), channel_id=1, replica_groups=mesh['bubble'=16,'panel'=16] {'bubble'}, dimensions={0}, use_global_device_ids=true | all-gather | bytes 8704 | tf_op jit(solution)/shard_map/all_gather | solution.py:75
  203.7 0.2 fusion.1
  203.8 0.2 fusion.32
  204.0 0.0 collective-permute-done.2
  204.0 0.0 collective-permute-done.3
  204.1 0.1 copy.37
  204.2 2.5 %gather_fusion.2 = bf16[192,128]{1,0:T(8,128)(2,1)S(1)} fusion(bf16[24,96,128]{2,1,0:T(8,128)(2,1)S(1)} %bitcast.100, s32[192]{0:T(256)S(1)} %reshape.62), kind=kCustom, calls=%fused_computation.2 | custom fusion | bytes 99840 | tf_op jit(solution)/shard_map/gather | solution.py:26
  206.7 0.1 select_bitcast_fusion
  206.8 4.5 %fusion.2 = f32[8,6,1,128,1]{3,2,4,1,0:T(1,128)S(1)} fusion(bf16[8,6,4,128,128]{4,3,2,1,0:T(8,128)(2,1)} %param.14, bf16[8,6,4,128,1]{3,2,1,0,4:T(4,128)(2,1)S(1)} %select_bitcast_fusion), kind=kOutput, calls=%fused_computation.9 | convolution fusion | flops 6291456 | bytes 6365184 | tf_op jit(solution)/shard_map/brsij,brsj->bri/dot_general | solution.py:29
  211.3 0.9 fusion.10
  212.3 0.7 bitcast_select_fusion
  (15 shorter events, 0.1 us)
Async XLA Ops:
  0.0 111.3 %copy-start = (bf16[8,6,128,128]{3,2,1,0:T(8,128)(2,1)S(1)}, bf16[8,6,128,128]{3,2,1,0:T(8,128)(2,1)}, u32[]{:S(2)}) copy-start(bf16[8,6,128,128]{3,2,1,0:T(8,128)(2,1)} %param.13) | copy-start | bytes 4718596
  20.2 83.7 %collective-permute-start = (bf16[8,12288]{1,0:T(8,128)(2,1)S(1)}, bf16[8,12288]{1,0:T(8,128)(2,1)S(1)}, u32[]{:S(2)}, u32[]{:S(2)}) collective-permute-start(bf16[8,12288]{1,0:T(8,128)(2,1)S(1)} %all_gather.12), channel_id=1, source_target_pairs={{0,16},{16,32},{32,48},{48,64},{64,80},{80,96},{96,112},{112,128},... | collective-permute-start | bytes 589832 | tf_op jit(solution)/shard_map/ppermute | solution.py:14
  24.0 79.9 %collective-permute-start.1 = (bf16[8,12288]{1,0:T(8,128)(2,1)S(1)}, bf16[8,12288]{1,0:T(8,128)(2,1)S(1)}, u32[]{:S(2)}, u32[]{:S(2)}) collective-permute-start(bf16[8,12288]{1,0:T(8,128)(2,1)S(1)} %all_gather.12), channel_id=1, source_target_pairs={{16,0},{32,16},{48,32},{64,48},{80,64},{96,80},{112,96},{128,112},... | collective-permute-start | bytes 589832 | tf_op jit(solution)/shard_map/ppermute | solution.py:15
  106.7 4.5 %copy-start.3 = (f32[8,768]{1,0:T(8,128)S(1)}, f32[8,768]{1,0:T(8,128)}, u32[]{:S(2)}) copy-start(f32[8,768]{1,0:T(8,128)} %param.12) | copy-start | bytes 73732
  111.3 1.0 copy-start.2
  111.3 27.0 %copy-start.4 = (bf16[8,16,768]{2,1,0:T(8,128)(2,1)S(1)}, bf16[8,16,768]{2,1,0:T(8,128)(2,1)}, u32[]{:S(2)}) copy-start(bf16[8,16,768]{2,1,0:T(8,128)(2,1)} %param.19) | copy-start | bytes 589828
  111.3 92.5 %copy-start.1 = (bf16[8,16,768]{2,1,0:T(8,128)(2,1)S(1)}, bf16[8,16,768]{2,1,0:T(8,128)(2,1)}, u32[]{:S(2)}) copy-start(bf16[8,16,768]{2,1,0:T(8,128)(2,1)} %param.20) | copy-start | bytes 589828
  128.8 75.2 %collective-permute-start.2 = (bf16[8,12288]{1,0:T(8,128)(2,1)S(1)}, bf16[8,12288]{1,0:T(8,128)(2,1)S(1)}, u32[]{:S(2)}, u32[]{:S(2)}) collective-permute-start(bf16[8,12288]{1,0:T(8,128)(2,1)S(1)} %all_gather.14), channel_id=1, source_target_pairs={{0,16},{16,32},{32,48},{48,64},{64,80},{80,96},{96,112},{112,128},... | collective-permute-start | bytes 589832 | tf_op jit(solution)/shard_map/ppermute | solution.py:14
  130.8 73.2 %collective-permute-start.3 = (bf16[8,12288]{1,0:T(8,128)(2,1)S(1)}, bf16[8,12288]{1,0:T(8,128)(2,1)S(1)}, u32[]{:S(2)}, u32[]{:S(2)}) collective-permute-start(bf16[8,12288]{1,0:T(8,128)(2,1)S(1)} %all_gather.14), channel_id=1, source_target_pairs={{16,0},{32,16},{48,32},{64,48},{80,64},{96,80},{112,96},{128,112},... | collective-permute-start | bytes 589832 | tf_op jit(solution)/shard_map/ppermute | solution.py:15
where the time goes:
time: 214 us; the launch traced here: 213 us
  blocking collectives  166 us (78%)
  starting transfers between devices  19.5 us (9%)
  matrix products  13.6 us (6%)
  local copies, waits for them, and re-layouts  7.75 us (4%)
  other arithmetic  5.75 us (3%)
    all_gather x2, blocking collectives, per_device(): all_moments = lax.all_gather(own_moments, 'bubble', axis=0, tiled=True)  74.5 us
    psum x2, blocking collectives, per_device(): own_moments = lax.psum(partial_value, 'panel')  55.7 us
    all_gather x2, blocking collectives, per_device(): panel_full = lax.all_gather(dens_bf, 'panel', axis=1, tiled=True)  35.9 us
    ppermute x2, starting transfers between devices, with_halo(): after = lax.ppermute(first, axis, down)  13.7 us
    dot_general x2, matrix products, near_field(): jnp.einsum('brsij,brsj->bri', near_vals, sources, preferred_element_type=...  9.02 us
    ppermute x2, starting transfers between devices, with_halo(): before = lax.ppermute(last, axis, up)  5.78 us
    gather x2, local copies, waits for them, and re-layouts, near_field(): sources = blocks[local_bubble, near_block]  5.03 us
  transfers between devices with their start and end apart: 4, of which 0 were waited for; matrix products, arithmetic and copies ran while one was open for 4% of the time, Pallas kernels for 0%

commit v1 on v0

--- a/solution.py
+++ b/solution.py
@@ -72,7 +72,10 @@
             "bki,bi->bk", moment_map, dens_bf, preferred_element_type=jnp.float32
         )
         own_moments = lax.psum(partial_value, "panel")
-        all_moments = lax.all_gather(own_moments, "bubble", axis=0, tiled=True)
+        all_moments = jnp.concatenate(
+            lax.all_to_all(jnp.stack([own_moments] * lax.axis_size("bubble")), "bubble", 0, 0),
+            axis=0,
+        )
         far_coeff = jnp.dot(kernel, all_moments, precision=lax.Precision.HIGHEST).astype(
             jnp.bfloat16
         )

time: 214 us -> 164 us (0.77)
  blocking collectives: 166 us -> 90.2 us
  starting transfers between devices: 19.5 us -> 36 us
  waiting for transfers between devices: 0.01 us -> 4.73 us
  local copies, waits for them, and re-layouts: 7.75 us -> 9.9 us
    all_gather x2 -> x0, blocking collectives: 74.5 us -> none  [per_device(): all_moments = lax.all_gather(own_moments, 'bubble', axis=0, tiled=True)]
    all_to_all x0 -> x2, starting transfers between devices: none -> 16.5 us  [per_device(): lax.all_to_all(jnp.stack([own_moments] * lax.axis_size('bubble')), 'bubbl...]
  transfers between devices with their start and end apart: 4 -> 6, of which waited for: 0 -> 3; matrix products, arithmetic and copies ran while one was open for 4% -> 7% of each run, Pallas kernels for 0% -> 0%
where the time goes in v1:
time: 164 us; the launch traced here: 162 us
  blocking collectives  90.2 us (55%)
  starting transfers between devices  36 us (22%)
  matrix products  13.7 us (8%)
  local copies, waits for them, and re-layouts  9.9 us (6%)
  other arithmetic  7.18 us (4%)
  waiting for transfers between devices  4.73 us (3%)
    psum x2, blocking collectives, per_device(): own_moments = lax.psum(partial_value, 'panel')  54.3 us
    all_gather x2, blocking collectives, per_device(): panel_full = lax.all_gather(dens_bf, 'panel', axis=1, tiled=True)  35.8 us
    all_to_all x2, starting transfers between devices, per_device(): lax.all_to_all(jnp.stack([own_moments] * lax.axis_size('bubble')), 'bubbl...  16.5 us
    ppermute x2, starting transfers between devices, with_halo(): after = lax.ppermute(first, axis, down)  12.3 us
    dot_general x2, matrix products, near_field(): jnp.einsum('brsij,brsj->bri', near_vals, sources, preferred_element_type=...  9.02 us
    ppermute x2, starting transfers between devices, with_halo(): before = lax.ppermute(last, axis, up)  7.17 us
    gather x2, local copies, waits for them, and re-layouts, near_field(): sources = blocks[local_bubble, near_block]  5.03 us
  transfers between devices with their start and end apart: 6, of which 3 were waited for; matrix products, arithmetic and copies ran while one was open for 7% of the time, Pallas kernels for 0%

profile of v1, /device:TPU:24, one launch (start us, length us, event | category | flops | bytes accessed | tf_op | source)
XLA Modules:
  0.0 161.9 jit_solution(8193922411422380527)
XLA Ops:
  0.0 0.9 convert_element_type.18
  0.9 19.4 %all_gather.6 = bf16[8,12288]{1,0:T(8,128)(2,1)S(1)} all-gather(bf16[8,768]{1,0:T(8,128)(2,1)S(1)} %convert_element_type.18), channel_id=1, replica_groups=mesh['bubble'=16,'panel'=16] {'panel'}, dimensions={1}, use_global_device_ids=true | all-gather | bytes 208896 | tf_op jit(solution)/shard_map/all_gather | solution.py:66
  20.2 3.8 %collective-permute-start = (bf16[8,12288]{1,0:T(8,128)(2,1)S(1)}, bf16[8,12288]{1,0:T(8,128)(2,1)S(1)}, u32[]{:S(2)}, u32[]{:S(2)}) collective-permute-start(bf16[8,12288]{1,0:T(8,128)(2,1)S(1)} %all_gather.6), channel_id=1, source_target_pairs={{0,16},{16,32},{32,48},{48,64},{64,80},{80,96},{96,112},{112,128},... | collective-permute-start | bytes 589832 | tf_op jit(solution)/shard_map/ppermute | solution.py:14
  24.0 6.2 %collective-permute-start.1 = (bf16[8,12288]{1,0:T(8,128)(2,1)S(1)}, bf16[8,12288]{1,0:T(8,128)(2,1)S(1)}, u32[]{:S(2)}, u32[]{:S(2)}) collective-permute-start(bf16[8,12288]{1,0:T(8,128)(2,1)S(1)} %all_gather.6), channel_id=1, source_target_pairs={{16,0},{32,16},{48,32},{64,48},{80,64},{96,80},{112,96},{128,112},... | collective-permute-start | bytes 589832 | tf_op jit(solution)/shard_map/ppermute | solution.py:15
  30.3 0.7 convert_bitcast_fusion
  31.0 1.1 fusion.18
  32.1 27.2 %psum.14 = f32[8,16]{1,0:T(8,128)S(1)} all-reduce(f32[8,16]{1,0:T(8,128)S(1)} %bitcast.103), channel_id=1, replica_groups=mesh['bubble'=16,'panel'=16] {'panel'}, use_global_device_ids=true, to_apply=%region_1.2 | all-reduce | flops 128 | bytes 1024 | tf_op jit(solution)/shard_map/psum | solution.py:74
  59.3 0.7 reshape.248
  60.0 8.4 %all-to-all-start = ((f32[16,1,128]{2,1,0:T(1,128)}), f32[16,1,128]{2,1,0:T(1,128)S(1)}, u32[]{:S(2)}, u32[]{:S(2)}) async-start(f32[16,1,128]{2,1,0:T(1,128)} %reshape.248), calls=%async_computation | async-start | bytes 16384 | tf_op jit(solution)/shard_map/all_to_all | solution.py:76
  68.4 0.8 copy.18
  69.2 0.6 gather_fusion.1
  69.8 0.1 copy.19
  69.8 0.2 slice_reduce_fusion
  70.0 0.7 slice_bitcast_fusion
  70.7 0.8 multiply_reduce_fusion
  71.5 0.8 iota_compare_fusion
  72.2 0.7 fusion.24
  73.1 0.7 broadcast_compare_fusion.1
  73.7 0.1 copy.17
  73.9 0.1 reshape.199
  74.0 1.5 all-to-all-done
  75.5 0.6 broadcast.226
  76.1 0.7 reduce.2
  76.9 0.2 fusion
  77.0 1.1 fusion.36
  78.2 0.1 copy.36
  78.3 2.5 %gather_fusion = bf16[192,128]{1,0:T(8,128)(2,1)S(1)} fusion(bf16[24,96,128]{2,1,0:T(8,128)(2,1)S(1)} %bitcast.97, s32[192]{0:T(256)S(1)} %reshape.199), kind=kCustom, calls=%fused_computation | custom fusion | bytes 99840 | tf_op jit(solution)/shard_map/gather | solution.py:26
  80.8 0.1 select_bitcast_fusion.1
  80.9 4.5 %fusion.4 = f32[8,6,1,128,1]{3,2,4,1,0:T(1,128)S(1)} fusion(bf16[8,6,4,128,128]{4,3,2,1,0:T(8,128)(2,1)} %param.14, bf16[8,6,4,128,1]{3,2,1,0,4:T(4,128)(2,1)S(1)} %select_bitcast_fusion.1), kind=kOutput, calls=%fused_computation.11 | convolution fusion | flops 6291456 | bytes 6365184 | tf_op jit(solution)/shard_map/brsij,brsj->bri/dot_general | solution.py:29
  85.5 0.9 fusion.16
  86.5 0.2 fusion.14
  86.7 27.1 %psum.15 = f32[8,16]{1,0:T(8,128)S(1)} all-reduce(f32[8,16]{1,0:T(8,128)S(1)} %bitcast.104), channel_id=1, replica_groups=mesh['bubble'=16,'panel'=16] {'panel'}, use_global_device_ids=true, to_apply=%region_2.3 | all-reduce | flops 128 | bytes 1024 | tf_op jit(solution)/shard_map/psum | solution.py:74
  113.8 0.7 reshape.250
  114.5 8.1 %all-to-all-start.1 = ((f32[16,1,128]{2,1,0:T(1,128)}), f32[16,1,128]{2,1,0:T(1,128)S(1)}, u32[]{:S(2)}, u32[]{:S(2)}) async-start(f32[16,1,128]{2,1,0:T(1,128)} %reshape.250), calls=%async_computation.1 | async-start | bytes 16384 | tf_op jit(solution)/shard_map/all_to_all | solution.py:76
  122.6 16.5 %all_gather.7 = bf16[8,12288]{1,0:T(8,128)(2,1)S(1)} all-gather(bf16[8,768]{1,0:T(8,128)(2,1)S(1)} %fusion.38), channel_id=1, replica_groups=mesh['bubble'=16,'panel'=16] {'panel'}, dimensions={1}, use_global_device_ids=true | all-gather | bytes 208896 | tf_op jit(solution)/shard_map/all_gather | solution.py:66
  139.1 3.4 %collective-permute-start.2 = (bf16[8,12288]{1,0:T(8,128)(2,1)S(1)}, bf16[8,12288]{1,0:T(8,128)(2,1)S(1)}, u32[]{:S(2)}, u32[]{:S(2)}) collective-permute-start(bf16[8,12288]{1,0:T(8,128)(2,1)S(1)} %all_gather.7), channel_id=1, source_target_pairs={{0,16},{16,32},{32,48},{48,64},{64,80},{80,96},{96,112},{112,128},... | collective-permute-start | bytes 589832 | tf_op jit(solution)/shard_map/ppermute | solution.py:14
  142.5 6.1 %collective-permute-start.3 = (bf16[8,12288]{1,0:T(8,128)(2,1)S(1)}, bf16[8,12288]{1,0:T(8,128)(2,1)S(1)}, u32[]{:S(2)}, u32[]{:S(2)}) collective-permute-start(bf16[8,12288]{1,0:T(8,128)(2,1)S(1)} %all_gather.7), channel_id=1, source_target_pairs={{16,0},{32,16},{48,32},{64,48},{80,64},{96,80},{112,96},{128,112},... | collective-permute-start | bytes 589832 | tf_op jit(solution)/shard_map/ppermute | solution.py:15
  148.6 0.7 reduce.3
  149.4 0.2 fusion.1
  149.5 0.2 fusion.34
  149.7 2.0 %collective-permute-done.2 = bf16[8,12288]{1,0:T(8,128)(2,1)S(1)} collective-permute-done((bf16[8,12288]{1,0:T(8,128)(2,1)S(1)}, bf16[8,12288]{1,0:T(8,128)(2,1)S(1)}, u32[]{:S(2)}, u32[]{:S(2)}) %collective-permute-start.2) | collective-permute-done | bytes 196640 | tf_op jit(solution)/shard_map/ppermute | solution.py:14
  151.8 1.2 collective-permute-done.3
  153.0 0.1 copy.37
  153.1 2.5 %gather_fusion.2 = bf16[192,128]{1,0:T(8,128)(2,1)S(1)} fusion(bf16[24,96,128]{2,1,0:T(8,128)(2,1)S(1)} %bitcast.96, s32[192]{0:T(256)S(1)} %reshape.199), kind=kCustom, calls=%fused_computation.2 | custom fusion | bytes 99840 | tf_op jit(solution)/shard_map/gather | solution.py:26
  155.6 0.1 select_bitcast_fusion
  155.7 4.5 %fusion.2 = f32[8,6,1,128,1]{3,2,4,1,0:T(1,128)S(1)} fusion(bf16[8,6,4,128,128]{4,3,2,1,0:T(8,128)(2,1)} %param.14, bf16[8,6,4,128,1]{3,2,1,0,4:T(4,128)(2,1)S(1)} %select_bitcast_fusion), kind=kOutput, calls=%fused_computation.9 | convolution fusion | flops 6291456 | bytes 6365184 | tf_op jit(solution)/shard_map/brsij,brsj->bri/dot_general | solution.py:29
  160.3 0.9 fusion.12
  161.2 0.7 bitcast_select_fusion
  (26 shorter events, 0.5 us)
Async XLA Ops:
  0.0 85.5 %copy-start = (bf16[8,6,128,128]{3,2,1,0:T(8,128)(2,1)S(1)}, bf16[8,6,128,128]{3,2,1,0:T(8,128)(2,1)}, u32[]{:S(2)}) copy-start(bf16[8,6,128,128]{3,2,1,0:T(8,128)(2,1)} %param.13) | copy-start | bytes 4718596
  20.2 57.9 %collective-permute-start = (bf16[8,12288]{1,0:T(8,128)(2,1)S(1)}, bf16[8,12288]{1,0:T(8,128)(2,1)S(1)}, u32[]{:S(2)}, u32[]{:S(2)}) collective-permute-start(bf16[8,12288]{1,0:T(8,128)(2,1)S(1)} %all_gather.6), channel_id=1, source_target_pairs={{0,16},{16,32},{32,48},{48,64},{64,80},{80,96},{96,112},{112,128},... | collective-permute-start | bytes 589832 | tf_op jit(solution)/shard_map/ppermute | solution.py:14
  24.0 54.1 %collective-permute-start.1 = (bf16[8,12288]{1,0:T(8,128)(2,1)S(1)}, bf16[8,12288]{1,0:T(8,128)(2,1)S(1)}, u32[]{:S(2)}, u32[]{:S(2)}) collective-permute-start(bf16[8,12288]{1,0:T(8,128)(2,1)S(1)} %all_gather.6), channel_id=1, source_target_pairs={{16,0},{32,16},{48,32},{64,48},{80,64},{96,80},{112,96},{128,112},... | collective-permute-start | bytes 589832 | tf_op jit(solution)/shard_map/ppermute | solution.py:15
  60.0 15.5 %all-to-all-start = ((f32[16,1,128]{2,1,0:T(1,128)}), f32[16,1,128]{2,1,0:T(1,128)S(1)}, u32[]{:S(2)}, u32[]{:S(2)}) async-start(f32[16,1,128]{2,1,0:T(1,128)} %reshape.248), calls=%async_computation | async-start | bytes 16384 | tf_op jit(solution)/shard_map/all_to_all | solution.py:76
  80.9 4.5 %copy-start.3 = (f32[8,768]{1,0:T(8,128)S(1)}, f32[8,768]{1,0:T(8,128)}, u32[]{:S(2)}) copy-start(f32[8,768]{1,0:T(8,128)} %param.12) | copy-start | bytes 73732
  85.4 1.0 copy-start.2
  85.4 1.0 copy-start.4
  85.4 64.1 %copy-start.1 = (bf16[8,16,768]{2,1,0:T(8,128)(2,1)S(1)}, bf16[8,16,768]{2,1,0:T(8,128)(2,1)}, u32[]{:S(2)}) copy-start(bf16[8,16,768]{2,1,0:T(8,128)(2,1)} %param.20) | copy-start | bytes 589828
  114.5 34.1 %all-to-all-start.1 = ((f32[16,1,128]{2,1,0:T(1,128)}), f32[16,1,128]{2,1,0:T(1,128)S(1)}, u32[]{:S(2)}, u32[]{:S(2)}) async-start(f32[16,1,128]{2,1,0:T(1,128)} %reshape.250), calls=%async_computation.1 | async-start | bytes 16384 | tf_op jit(solution)/shard_map/all_to_all | solution.py:76
  139.1 12.6 %collective-permute-start.2 = (bf16[8,12288]{1,0:T(8,128)(2,1)S(1)}, bf16[8,12288]{1,0:T(8,128)(2,1)S(1)}, u32[]{:S(2)}, u32[]{:S(2)}) collective-permute-start(bf16[8,12288]{1,0:T(8,128)(2,1)S(1)} %all_gather.7), channel_id=1, source_target_pairs={{0,16},{16,32},{32,48},{48,64},{64,80},{80,96},{96,112},{112,128},... | collective-permute-start | bytes 589832 | tf_op jit(solution)/shard_map/ppermute | solution.py:14
  142.5 10.5 %collective-permute-start.3 = (bf16[8,12288]{1,0:T(8,128)(2,1)S(1)}, bf16[8,12288]{1,0:T(8,128)(2,1)S(1)}, u32[]{:S(2)}, u32[]{:S(2)}) collective-permute-start(bf16[8,12288]{1,0:T(8,128)(2,1)S(1)} %all_gather.7), channel_id=1, source_target_pairs={{16,0},{32,16},{48,32},{64,48},{80,64},{96,80},{112,96},{128,112},... | collective-permute-start | bytes 589832 | tf_op jit(solution)/shard_map/ppermute | solution.py:15
